TPU v7x, 512 devices: a whole 4x8x8 slice. The times are simulated.
512 devices in a mesh: seq: 64 (over y, z), head: 8 (over x, core).
Axes of the slice: x: 4, y: 8, z: 8, core: 2. Of those that a mesh axis runs over, the one named last changes fastest.
Arguments:
- layer_input_rows: bfloat16 [8192, 4096], P('seq', 'head'), may hold values from -6 to 6
- filter_input_channels: bfloat16 [8192, 8192], P('seq', 'head'), may hold values from -6 to 6
- gate_input_channels: bfloat16 [8192, 8192], P('seq', 'head'), may hold values from -6 to 6
- state_input_vectors: bfloat16 [8192, 128], P('seq'), may hold values from -3 to 3
- state_output_vectors: bfloat16 [8192, 128], P('seq'), may hold values from -3 to 3
- decay_logarithm: float32 [8192, 64], P('seq', 'head'), may hold values from -0.7 to 0, as said below
- filter_tap_weight: bfloat16 [4, 8192], P(None, 'head'), may hold values from -3 to 3
- head_skip_gain: float32 [64], P('head'), may hold values from 0.5 to 1.5
- gated_norm_gain: float32 [8192], P('head'), may hold values from 0.1 to 1.9
- adapter_down_in: bfloat16 [4096, 32], P('head'), may hold values from -0.09375 to 0.09375
- adapter_up_in: bfloat16 [2, 32, 8192], P(None, None, 'head'), may hold values from -1 to 1
- adapter_down_out: bfloat16 [8192, 32], P('head'), may hold values from -0.0625 to 0.0625
- adapter_up_out: bfloat16 [32, 4096], P(None, 'head'), may hold values from -1 to 1
- output_gradient: bfloat16 [8192, 4096], P('seq', 'head'), may hold values from -6 to 6
- base_path_gradient: bfloat16 [8192, 8192], P('seq', 'head'), may hold values from -6 to 6
Outputs:
- grad_conv_in: bfloat16 [8192, 8192], P('seq', 'head')
- grad_gate_in: bfloat16 [8192, 8192], P('seq', 'head')
- grad_state_b: float32 [8192, 128], P(('seq', 'head'))
- grad_state_c: float32 [8192, 128], P(('seq', 'head'))
- grad_log_decay: float32 [8192, 64], P('seq', 'head')
- grad_layer_in: bfloat16 [8192, 4096], P('seq', 'head')
- grad_lora_a_in: float32 [4096, 32], P('head')
- grad_lora_b_in: float32 [2, 32, 8192], P(None, None, 'head')
- grad_lora_a_out: float32 [8192, 32], P('head')
- grad_lora_b_out: float32 [32, 4096], P(None, 'head')
Inputs may be any that keep to these rules, and one draw needn't show every extreme that they name: `decay_logarithm`: each entry is the logarithm of a decay factor between 0 and 1.
All inputs are finite; a program needn't handle non-finite values.
Results may differ from a plain program's by a relative error of at most 0.0017.
Values may be sent and summed in bfloat16 or wider, within the bound.
A program may use at most 128 MiB of HBM per device.

v0:
```python
import jax
import jax.numpy as jnp
from jax import lax
from jax.sharding import PartitionSpec as P

HDIM = 128
NSTATE = 128
BLOCK = 256
PRECISE_PRODUCT = lax.Precision.HIGHEST
ADAPTER_SCALE = 2.0
NORM_EPS = 1e-05


def passed_along(x, axis, by):
    devices = lax.axis_size(axis)
    pairs = [(i, i + by) for i in range(devices) if 0 <= i + by < devices]
    return lax.ppermute(x, axis, pairs)


def prefix(part, axis, combine, identity, reverse):
    count = lax.axis_size(axis)
    place = lax.axis_index(axis)
    ahead = count - 1 - place if reverse else place
    gathered = jax.tree.map(lambda a: lax.all_gather(a, axis), part)
    state = jax.tree.map(lambda a, e: jnp.zeros_like(a) + jnp.asarray(e, a.dtype), part, identity)

    def one(turn, state):
        source = count - 1 - turn if reverse else turn
        return combine(
            state, jax.tree.map(lambda a: lax.dynamic_index_in_dim(a, source, 0, False), gathered)
        )

    return lax.fori_loop(0, ahead, one, state)


def block_pass(activated, b_float, c_float, logarithm_increments, start_state, block_rows):
    tok_rows, head_count, head_width = activated.shape
    block_count = tok_rows // block_rows
    state_width = b_float.shape[1]
    causal = (jnp.arange(block_rows)[:, None] >= jnp.arange(block_rows)[None, :])[None, :, :]

    def advance(carried_state, block_items):
        x_block, b_block, c_block, l_block = block_items
        cum_decay = jnp.cumsum(l_block, axis=0)
        cum_heads = cum_decay.T
        decay_gap = jnp.where(causal, cum_heads[:, :, None] - cum_heads[:, None, :], 0.0)
        decays = jnp.where(causal, jnp.exp(decay_gap), 0.0)
        scores = jnp.dot(c_block, b_block.T, precision=PRECISE_PRODUCT)
        weights = decays * scores[None, :, :]
        inner_out = jnp.einsum("hts,shp->thp", weights, x_block, precision=PRECISE_PRODUCT)
        outer_out = jnp.exp(cum_decay)[:, :, None] * jnp.einsum(
            "tn,hnp->thp", c_block, carried_state, precision=PRECISE_PRODUCT
        )
        to_end = jnp.exp(cum_decay[-1][None, :] - cum_decay)
        fresh_state = jnp.einsum(
            "sn,shp->hnp", b_block, x_block * to_end[:, :, None], precision=PRECISE_PRODUCT
        )
        next_state = jnp.exp(cum_decay[-1])[:, None, None] * carried_state + fresh_state
        return (next_state, inner_out + outer_out)

    block_items = (
        activated.reshape(block_count, block_rows, head_count, head_width),
        b_float.reshape(block_count, block_rows, state_width),
        c_float.reshape(block_count, block_rows, state_width),
        logarithm_increments.reshape(block_count, block_rows, head_count),
    )
    end_state, outputs = lax.scan(advance, start_state, block_items)
    return (outputs.reshape(tok_rows, head_count, head_width), end_state)


def carried(c_float, logarithm_increments, state_in):
    cum_decay = jnp.cumsum(logarithm_increments, axis=0)
    outer_out = jnp.exp(cum_decay)[:, :, None] * jnp.einsum(
        "tn,hnp->thp", c_float, state_in, precision=PRECISE_PRODUCT
    )
    passed = jnp.exp(cum_decay[-1])[:, None, None] * state_in
    return (outer_out, passed)


def end_state(activated, b_float, logarithm_increments):
    cum_decay = jnp.cumsum(logarithm_increments, axis=0)
    to_end = jnp.exp(cum_decay[-1][None, :] - cum_decay)
    return jnp.einsum(
        "sn,shp->hnp", b_float, activated * to_end[:, :, None], precision=PRECISE_PRODUCT
    )


def chain_step(earlier, later_part):
    return (
        earlier[0] + later_part[0],
        jnp.exp(later_part[0])[:, None, None] * earlier[1] + later_part[1],
    )


def body(
    layer_input_rows,
    filter_input_channels,
    gate_input_channels,
    state_input_vectors,
    state_output_vectors,
    decay_logarithm,
    filter_tap_weight,
    head_skip_gain,
    gated_norm_gain,
    adapter_down_in,
    adapter_up_in,
    adapter_down_out,
    adapter_up_out,
    output_gradient,
    base_path_gradient,
):
    tok_rows, chan_width = filter_input_channels.shape
    head_count = decay_logarithm.shape[1]
    rim_rows = filter_tap_weight.shape[0] - 1
    block_rows = min(BLOCK, tok_rows)
    row_total_count = tok_rows * lax.axis_size("seq")
    all_channels = chan_width * lax.axis_size("head")
    taps = filter_tap_weight.astype(jnp.float32)
    before = passed_along(filter_input_channels[tok_rows - rim_rows :], "seq", 1)
    padded = jnp.concatenate([before, filter_input_channels], axis=0).astype(jnp.float32)
    pre_act = padded[0:tok_rows] * taps[0][None, :]
    for offset in range(1, rim_rows + 1):
        pre_act = pre_act + padded[offset : offset + tok_rows] * taps[offset][None, :]
    act_heads = jax.nn.silu(pre_act).reshape(tok_rows, head_count, HDIM)
    b_float = state_input_vectors.astype(jnp.float32)
    c_float = state_output_vectors.astype(jnp.float32)
    zero_state = jnp.zeros((head_count, NSTATE, HDIM), jnp.float32)
    zero_decay = jnp.zeros((head_count,), jnp.float32)

    def local_pass(activated, b_part, c_part, logarithm_increments):
        return block_pass(activated, b_part, c_part, logarithm_increments, zero_state, block_rows)

    (inner_out, fresh_state), pull_local = jax.vjp(
        local_pass, act_heads, b_float, c_float, decay_logarithm
    )
    total_decay = jnp.sum(decay_logarithm, axis=0)
    _, state_in = prefix(
        (total_decay, fresh_state), "seq", chain_step, (zero_decay, zero_state), False
    )
    (outer_out, _), pull_carry = jax.vjp(carried, c_float, decay_logarithm, state_in)
    ssd_out = inner_out + outer_out + head_skip_gain[None, :, None] * act_heads
    mixer_out = ssd_out.reshape(tok_rows, chan_width)
    gate_float = gate_input_channels.astype(jnp.float32)
    gate_sig = jax.nn.sigmoid(gate_float)
    gated_out = mixer_out * gate_float * gate_sig
    square_part = jnp.sum(gated_out * gated_out, axis=1)
    scaled = gated_out * gated_norm_gain[None, :]
    down_out_factor = adapter_down_out.astype(jnp.float32)
    square_sum = lax.psum(square_part, "head")
    inv_rms = lax.rsqrt(square_sum / all_channels + NORM_EPS)
    normed = scaled * inv_rms[:, None]
    low_out = lax.psum(jnp.dot(normed, down_out_factor, precision=PRECISE_PRODUCT), "head")
    reverse_out_grad = lax.psum(
        jnp.dot(output_gradient, adapter_up_out.T, preferred_element_type=jnp.float32), "head"
    )
    normalized_gradient = base_path_gradient.astype(jnp.float32) + ADAPTER_SCALE * jnp.dot(
        reverse_out_grad, down_out_factor.T, precision=PRECISE_PRODUCT
    )
    weighted = normalized_gradient * gated_norm_gain[None, :]
    dot_total = lax.psum(jnp.sum(weighted * gated_out, axis=1), "head")
    grad_gated = (
        inv_rms[:, None] * weighted
        - gated_out * (inv_rms * inv_rms * inv_rms * dot_total / all_channels)[:, None]
    )
    grad_mixer = grad_gated * gate_float * gate_sig
    grad_gate = grad_gated * mixer_out * gate_sig * (1.0 + gate_float * (1.0 - gate_sig))
    grad_ssd = grad_mixer.reshape(tok_rows, head_count, HDIM)
    cum_decay = jnp.cumsum(decay_logarithm, axis=0)
    local_grad = jnp.einsum(
        "tn,thp->hnp", c_float, grad_ssd * jnp.exp(cum_decay)[:, :, None], precision=PRECISE_PRODUCT
    )
    _, state_grad = prefix(
        (total_decay, local_grad), "seq", chain_step, (zero_decay, zero_state), True
    )
    grad_act, grad_b, grad_c, grad_steps = pull_local((grad_ssd, state_grad))
    carry_c, carry_steps, _ = pull_carry((grad_ssd, state_grad))
    grad_c = grad_c + carry_c
    grad_steps = grad_steps + carry_steps
    grad_act = grad_act + head_skip_gain[None, :, None] * grad_ssd
    pre_sig = jax.nn.sigmoid(pre_act)
    grad_pre = grad_act.reshape(tok_rows, chan_width) * pre_sig * (1.0 + pre_act * (1.0 - pre_sig))
    after = passed_along(grad_pre[:rim_rows], "seq", -1)
    extended = jnp.concatenate([grad_pre, after], axis=0)
    grad_conv = extended[rim_rows : rim_rows + tok_rows] * taps[0][None, :]
    for offset in range(1, rim_rows + 1):
        grad_conv = (
            grad_conv
            + extended[rim_rows - offset : rim_rows - offset + tok_rows] * taps[offset][None, :]
        )
    grad_b_rows, grad_c_rows = (
        lax.psum_scatter(grad_b, "head", scatter_dimension=0, tiled=True),
        lax.psum_scatter(grad_c, "head", scatter_dimension=0, tiled=True),
    )
    reduced_input = lax.psum(
        jnp.dot(layer_input_rows, adapter_down_in, preferred_element_type=jnp.float32), "head"
    )
    up_in_factor = adapter_up_in.astype(jnp.float32)
    back_part = jnp.dot(grad_conv, up_in_factor[0].T, precision=PRECISE_PRODUCT) + jnp.dot(
        grad_gate, up_in_factor[1].T, precision=PRECISE_PRODUCT
    )
    reverse_in_grad = lax.psum(back_part, "head")
    layer_gradient_fn = (
        ADAPTER_SCALE
        * jnp.dot(reverse_in_grad, adapter_down_in.astype(jnp.float32).T, precision=PRECISE_PRODUCT)
    ).astype(jnp.bfloat16)
    averaging_scale = ADAPTER_SCALE / row_total_count
    grad_a_in, grad_b_in, grad_a_out, grad_b_out = lax.psum(
        (
            averaging_scale
            * jnp.dot(
                layer_input_rows.astype(jnp.float32).T, reverse_in_grad, precision=PRECISE_PRODUCT
            ),
            averaging_scale
            * jnp.stack(
                [
                    jnp.dot(reduced_input.T, grad_conv, precision=PRECISE_PRODUCT),
                    jnp.dot(reduced_input.T, grad_gate, precision=PRECISE_PRODUCT),
                ]
            ),
            averaging_scale * jnp.dot(normed.T, reverse_out_grad, precision=PRECISE_PRODUCT),
            averaging_scale
            * jnp.dot(low_out.T, output_gradient.astype(jnp.float32), precision=PRECISE_PRODUCT),
        ),
        "seq",
    )
    return (
        grad_conv.astype(jnp.bfloat16),
        grad_gate.astype(jnp.bfloat16),
        grad_b_rows,
        grad_c_rows,
        grad_steps,
        layer_gradient_fn,
        grad_a_in,
        grad_b_in,
        grad_a_out,
        grad_b_out,
    )


def solution(mesh):
    in_specs = (
        P("seq", "head"),
        P("seq", "head"),
        P("seq", "head"),
        P("seq", None),
        P("seq", None),
        P("seq", "head"),
        P(None, "head"),
        P("head"),
        P("head"),
        P("head", None),
        P(None, None, "head"),
        P("head", None),
        P(None, "head"),
        P("seq", "head"),
        P("seq", "head"),
    )
    out_specs = (
        P("seq", "head"),
        P("seq", "head"),
        P(("seq", "head"), None),
        P(("seq", "head"), None),
        P("seq", "head"),
        P("seq", "head"),
        P("head", None),
        P(None, None, "head"),
        P("head", None),
        P(None, "head"),
    )
    return jax.shard_map(body, mesh=mesh, in_specs=in_specs, out_specs=out_specs, check_vma=False)
```

profile of v0, /device:TPU:2, one launch (start us, length us, event | category | flops | bytes accessed | tf_op | source)
XLA Modules:
  0.0 900.4 jit_solution(9360454591310786965)
XLA Ops:
  8.1 4.3 collective-permute-start
  19.9 1.3 dynamic-slice
  22.1 151.3 %all-reduce.3 = f32[512]{0:T(512)S(1)} all-reduce(f32[512]{0:T(512)S(1)} %dynamic-update-slice), channel_id=2, replica_groups=mesh['seq'=64,'head'=8] {'seq'}, use_global_device_ids=true, to_apply=%add.3 | all-reduce | flops 512 | bytes 4096
  175.6 21.8 %psum.71 = f32[128,32]{0,1:T(8,128)} all-reduce(f32[128,32]{0,1:T(8,128)S(1)} %fusion.89), channel_id=1, replica_groups=mesh['seq'=64,'head'=8] {'head'}, use_global_device_ids=true, to_apply=%region_6.7 | all-reduce | flops 4096 | bytes 32768 | tf_op jit(solution)/shard_map/psum | solution.py:153
  199.4 48.0 %all-gather.6.cloned.1.call-done = f32[512,128,128]{2,1,0:T(8,128)} async-done(((f32[8,128,128]{2,1,0:T(8,128)}), f32[512,128,128]{2,1,0:T(8,128)}) %all-gather.6.cloned.1.call-update) | async-done | bytes 33554448 | tf_op jit(solution)/shard_map/all_gather | solution.py:24
  248.1 1.3 convolution_bitcast_fusion.2
  249.4 2.1 fusion.6
  251.8 3.2 multiply_reduce_fusion.7
  254.9 12.4 %all-reduce.6 = (f32[128]{0:T(128)}, f32[128]{0:T(128)}) all-reduce(f32[128]{0:T(128)} %get-tuple-element.524, f32[128]{0:T(128)} %get-tuple-element.523), channel_id=1, replica_groups=mesh['seq'=64,'head'=8] {'head'}, use_global_device_ids=true, to_apply=%region_8.9 | all-reduce | flops 256 | bytes 2048 | tf_op jit(solution)/shard_map/psum | solution.py:160
  268.0 2.8 fusion.81
  270.8 1.2 copy.139
  272.0 1.9 convolution_bitcast_fusion.1
  274.0 2.0 copy.140
  276.1 1.3 broadcast_bitcast_fusion
  277.4 1.5 fusion.90
  278.9 1.6 convolution_bitcast_fusion.9
  280.5 1.7 convolution_bitcast_fusion.8
  282.9 2.0 fusion.43
  285.7 1.5 fusion.41
  287.3 2.2 convolution_multiply_fusion.2
  289.6 280.1 %all-gather.8.cloned.1.call-done = f32[512,128,128]{2,1,0:T(8,128)} async-done(((f32[8,128,128]{2,1,0:T(8,128)}), f32[512,128,128]{2,1,0:T(8,128)}) %all-gather.8.cloned.1.call-update) | async-done | bytes 33554448 | tf_op jit(solution)/shard_map/all_gather | solution.py:24
  569.8 120.5 %while.21 = (s32[]{:T(128)}, f32[8,128,128]{2,1,0:T(8,128)S(1)}, s32[]{:T(128)}, f32[64,8]{1,0:T(8,128)}, f32[64,8,128,128]{3,2,1,0:T(8,128)}, /*index=5*/s32[]{:T(128)}, s32[]{:T(128)}, s32[]{:T(128)}, s32[]{:T(128)}) while((s32[]{:T(128)}, f32[8,128,128]{2,1,0:T(8,128)S(1)}, s32[]{:T(128)}, f32[64,8]{1,0:T(8,128)}, ...), condition=%wide.region_10.11_spmd, body=%wide.region_9.10_spmd.sunk | while | flops 262150 | bytes 1573115 | solution.py:33
  570.5 1.2 bitcast_add_fusion.6
  572.4 1.2 bitcast_add_fusion.6
  574.3 1.2 bitcast_add_fusion.6
  576.2 1.2 bitcast_add_fusion.6
  578.1 1.2 bitcast_add_fusion.6
  587.7 1.2 bitcast_add_fusion.6
  589.6 1.2 bitcast_add_fusion.6
  591.5 1.2 bitcast_add_fusion.6
  595.3 1.2 bitcast_add_fusion.6
  597.2 1.2 bitcast_add_fusion.6
  603.0 1.2 bitcast_add_fusion.6
  690.5 1.7 convolution_bitcast_fusion.10
  693.8 1.6 fusion.2
  695.6 1.4 add_multiply_fusion
  697.0 1.3 collective-permute-start.1
  699.2 3.5 collective-permute-done.1
  702.7 1.7 fusion.83
  704.3 1.2 fusion.65
  705.5 1.2 convolution_add_fusion.3
  706.8 21.9 %all-reduce.5 = (f32[128,32]{0,1:T(8,128)S(1)}, f32[128,32]{0,1:T(8,128)S(1)}, f32[128,32]{0,1:T(8,128)S(1)}) all-reduce(f32[128,32]{0,1:T(8,128)S(1)} %convolution_add_fusion.3, f32[128,32]{0,1:T(8,128)} %fusion.90, f32[128,32]{0,1:T(8,128)S(1)} %fusion.41), channel_id=1, replica_groups=mesh['seq'=64,'head'=8] {'head'}, use_global_device_ids=true, to_apply=%region_24.25 | all-reduce | flops 12288 | bytes 98304 | tf_op jit(solution)/shard_map/psum | solution.py:201
  736.6 1.7 fusion.7
  738.4 149.3 %all-reduce.9.cloned.1.call-done = (f32[512,32]{0,1:T(8,128)}, f32[2,32,1024]{2,1,0:T(8,128)}, f32[1024,32]{0,1:T(8,128)}, f32[32,512]{1,0:T(8,128)}) async-done(((f32[512,32]{0,1:T(8,128)}, f32[2,32,1024]{2,1,0:T(8,128)}, f32[1024,32]{0,1:T(8,128)}, f32[32,512]{1,0:T(8,128)}), (f32[512,32]{0,1:T(8,128)}, f32[2,32,1024]{2,1,0:T(8,128)}, f32[1024,32]{0,1:T(8,128)}, ...) | async-done | bytes 524304 | tf_op jit(solution)/shard_map/psum | solution.py:207
  887.7 1.5 copy.191
  889.2 1.7 copy.192
  890.8 1.6 copy.193
  892.4 1.5 copy.194
  (213 shorter events, 132.5 us)
Async XLA Ops:
  7.2 167.5 %copy-start = (bf16[128,512]{1,0:T(8,128)(2,1)S(1)}, bf16[128,512]{1,0:T(8,128)(2,1)}, u32[]{:S(2)}) copy-start(bf16[128,512]{1,0:T(8,128)(2,1)} %param.32) | copy-start | bytes 393220
  7.2 277.7 %copy-start.4 = (bf16[128,128]{1,0:T(8,128)(2,1)S(1)}, bf16[128,128]{1,0:T(8,128)(2,1)}, u32[]{:S(2)}) copy-start(bf16[128,128]{1,0:T(8,128)(2,1)} %param.22) | copy-start | bytes 98308
  7.2 685.7 %copy-start.3 = (bf16[128,128]{1,0:T(8,128)(2,1)S(1)}, bf16[128,128]{1,0:T(8,128)(2,1)}, u32[]{:S(2)}) copy-start(bf16[128,128]{1,0:T(8,128)(2,1)} %param.23) | copy-start | bytes 98308
  7.2 270.2 %copy-start.5 = (bf16[128,512]{1,0:T(8,128)(2,1)S(1)}, bf16[128,512]{1,0:T(8,128)(2,1)}, u32[]{:S(2)}) copy-start(bf16[128,512]{1,0:T(8,128)(2,1)} %param.19) | copy-start | bytes 393220
  7.2 240.2 %all-gather.6.cloned.1.call-start = ((), (), s32[]{:S(2)}) async-start(), calls=%async_computation.4 | async-start | bytes 34078720 | tf_op jit(solution)/shard_map/all_gather | solution.py:24
  8.1 6.5 collective-permute-start
  13.2 3.5 copy-start.10
  13.2 3.5 copy-start.11
  13.2 3.5 copy-start.12
  13.2 3.5 copy-start.13
  14.2 159.3 %copy-start.9 = (f32[128,8]{0,1:T(8,128)}, f32[128,8]{0,1:T(8,128)S(1)}, u32[]{:S(2)}) copy-start(f32[128,8]{0,1:T(8,128)S(1)} %copy.132) | copy-start | bytes 12292
  14.5 182.8 %copy-start.6 = (f32[128,8]{0,1:T(8,128)}, f32[128,8]{0,1:T(8,128)S(1)}, u32[]{:S(2)}) copy-start(f32[128,8]{0,1:T(8,128)S(1)} %get-tuple-element.573) | copy-start | bytes 12292
  14.5 237.0 %copy-start.8 = (f32[128,8]{0,1:T(8,128)}, f32[128,8]{0,1:T(8,128)S(1)}, u32[]{:S(2)}) copy-start(f32[128,8]{0,1:T(8,128)S(1)} %get-tuple-element.574) | copy-start | bytes 12292
  19.1 550.6 %all-gather.8.cloned.1.call-start = ((), (), s32[]{:S(2)}) async-start(), calls=%async_computation.5 | async-start | bytes 34078720 | tf_op jit(solution)/shard_map/all_gather | solution.py:24
  173.6 78.0 %copy-start.7 = (f32[8,128]{1,0:T(8,128)}, f32[8,128]{1,0:T(8,128)S(1)}, u32[]{:S(2)}) copy-start(f32[8,128]{1,0:T(8,128)S(1)} %copy.129) | copy-start | bytes 12292
  247.5 0.6 copy-start.14
  251.7 16.2 %copy-start.2 = (f32[128,1024]{1,0:T(8,128)}, f32[128,1024]{1,0:T(8,128)S(1)}, u32[]{:S(2)}) copy-start(f32[128,1024]{1,0:T(8,128)S(1)} %copy.138) | copy-start | bytes 1572868
  254.9 15.9 %copy-start.1 = (f32[128,1024]{1,0:T(8,128)}, f32[128,1024]{1,0:T(8,128)S(1)}, u32[]{:S(2)}) copy-start(f32[128,1024]{1,0:T(8,128)S(1)} %get-tuple-element.560) | copy-start | bytes 1572868
  268.0 2.8 copy-start.15
  276.0 462.3 %reduce-scatter.5.cloned.1.call-start = ((), (), s32[]{:S(2)}) async-start(), calls=%async_computation.3 | async-start | bytes 73728 | tf_op jit(solution)/shard_map/reduce_scatter | solution.py:192
  289.5 448.9 %reduce-scatter.3.cloned.1.call-start = ((), (), s32[]{:S(2)}) async-start(), calls=%async_computation.2 | async-start | bytes 73728 | tf_op jit(solution)/shard_map/reduce_scatter | solution.py:191
  697.0 5.6 collective-permute-start.1
  699.1 188.6 %all-reduce.9.cloned.1.call-start = ((), (), s32[]{:S(2)}) async-start(), calls=%async_computation.6 | async-start | bytes 1048576 | tf_op jit(solution)/shard_map/psum | solution.py:207
Sparse Core Ops, SparseCore 0:
  19.2 228.1 all-gather.5
  276.1 293.5 all-gather.7
  573.1 30.7 reduce-scatter.4
  699.2 25.5 reduce-scatter.2
  732.0 155.6 all-reduce.8
where the time goes:
time: 907 us; the launch traced here: 900 us
  waiting for transfers between devices  481 us (53%)
  blocking collectives  207 us (23%)
  other arithmetic  90.8 us (10%)
  local copies, waits for them, and re-layouts  63.6 us (7%)
  matrix products  35.3 us (4%)
  between operations  14.8 us (2%)
    all_gather x2, waiting for transfers between devices, prefix(): gathered = jax.tree.map(lambda a: lax.all_gather(a, axis), part)  328 us
    unnamed x1, blocking collectives  151 us
    psum x1, waiting for transfers between devices, body(): lax.psum((averaging_scale * jnp.dot(layer_input_rows.astype(jnp.float32)....  149 us
    add x63, other arithmetic, chain_step(): jnp.exp(later_part[0])[:, None, None] * earlier[1] + later_part[1]  74.8 us
    exp x63, local copies, waits for them, and re-layouts, chain_step(): jnp.exp(later_part[0])[:, None, None] * earlier[1] + later_part[1]  44 us
    psum x1, blocking collectives, body(): reverse_in_grad = lax.psum(back_part, 'head')  21.9 us
    psum x1, blocking collectives, body(): lax.psum(jnp.dot(output_gradient, adapter_up_out.T, preferred_element_typ...  21.8 us
  transfers between devices with their start and end apart: 7, of which 4 were waited for; matrix products, arithmetic and copies ran while one was open for 18% of the time, Pallas kernels for 0%

commit v1 on v0

--- a/solution.py
+++ b/solution.py
@@ -9,6 +9,14 @@
 PRECISE_PRODUCT = lax.Precision.HIGHEST
 ADAPTER_SCALE = 2.0
 NORM_EPS = 1e-05
+
+
+def added_up(block, axis):
+    size, result = (lax.axis_size(axis), block)
+    for far in [1 << k for k in range(size.bit_length() - 1)]:
+        route = [(i, i ^ far) for i in range(size)]
+        result = result + lax.ppermute(result, axis, route)
+    return result
 
 
 def passed_along(x, axis, by):
@@ -198,7 +206,7 @@
     back_part = jnp.dot(grad_conv, up_in_factor[0].T, precision=PRECISE_PRODUCT) + jnp.dot(
         grad_gate, up_in_factor[1].T, precision=PRECISE_PRODUCT
     )
-    reverse_in_grad = lax.psum(back_part, "head")
+    reverse_in_grad = added_up(back_part, "head")
     layer_gradient_fn = (
         ADAPTER_SCALE
         * jnp.dot(reverse_in_grad, adapter_down_in.astype(jnp.float32).T, precision=PRECISE_PRODUCT)

time: 907 us -> 945 us (1.042)
  waiting for transfers between devices: 481 us -> 500 us
    psum x1, waiting for transfers between devices: 149 us -> 163 us  [body(): lax.psum((averaging_scale * jnp.dot(layer_input_rows.astype(jnp.float32)....]
    psum x1, blocking collectives: 12.4 us -> 24.4 us  [body(): dot_total = lax.psum(jnp.sum(weighted * gated_out, axis=1), 'head')]
    psum x1, blocking collectives: 21.9 us -> 12.4 us  [body(): square_sum = lax.psum(square_part, 'head')]
  transfers between devices with their start and end apart: 7 -> 10, of which waited for: 4 -> 8; matrix products, arithmetic and copies ran while one was open for 18% -> 18% of each run, Pallas kernels for 0% -> 0%
where the time goes in v1:
time: 945 us; the launch traced here: 938 us
  waiting for transfers between devices  500 us (53%)
  blocking collectives  210 us (22%)
  other arithmetic  92.4 us (10%)
  local copies, waits for them, and re-layouts  64.2 us (7%)
  matrix products  40.7 us (4%)
  between operations  14.8 us (2%)
  starting transfers between devices  14.1 us (1%)
    all_gather x2, waiting for transfers between devices, prefix(): gathered = jax.tree.map(lambda a: lax.all_gather(a, axis), part)  326 us
    psum x1, waiting for transfers between devices, body(): lax.psum((averaging_scale * jnp.dot(layer_input_rows.astype(jnp.float32)....  163 us
    unnamed x1, blocking collectives  151 us
    add x63, other arithmetic, chain_step(): jnp.exp(later_part[0])[:, None, None] * earlier[1] + later_part[1]  74.8 us
    exp x63, local copies, waits for them, and re-layouts, chain_step(): jnp.exp(later_part[0])[:, None, None] * earlier[1] + later_part[1]  44 us
    psum x1, blocking collectives, body(): dot_total = lax.psum(jnp.sum(weighted * gated_out, axis=1), 'head')  24.4 us
    psum x1, blocking collectives, body(): lax.psum(jnp.dot(output_gradient, adapter_up_out.T, preferred_element_typ...  21.8 us
  transfers between devices with their start and end apart: 10, of which 8 were waited for; matrix products, arithmetic and copies ran while one was open for 18% of the time, Pallas kernels for 0%

profile of v1, /device:TPU:2, one launch (start us, length us, event | category | flops | bytes accessed | tf_op | source)
XLA Modules:
  0.0 938.1 jit_solution(5055806395263022290)
XLA Ops:
  8.1 4.3 collective-permute-start
  19.9 1.3 dynamic-slice
  22.1 151.3 %all-reduce.3 = f32[512]{0:T(512)S(1)} all-reduce(f32[512]{0:T(512)S(1)} %dynamic-update-slice), channel_id=2, replica_groups=mesh['seq'=64,'head'=8] {'seq'}, use_global_device_ids=true, to_apply=%add.3 | all-reduce | flops 512 | bytes 4096
  175.6 21.8 %psum.64 = f32[128,32]{0,1:T(8,128)} all-reduce(f32[128,32]{0,1:T(8,128)S(1)} %fusion.91), channel_id=1, replica_groups=mesh['seq'=64,'head'=8] {'head'}, use_global_device_ids=true, to_apply=%region_6.7 | all-reduce | flops 4096 | bytes 32768 | tf_op jit(solution)/shard_map/psum | solution.py:161
  198.3 1.7 fusion.92
  201.1 46.3 %all-gather.6.cloned.1.call-done = f32[512,128,128]{2,1,0:T(8,128)} async-done(((f32[8,128,128]{2,1,0:T(8,128)}), f32[512,128,128]{2,1,0:T(8,128)}) %all-gather.6.cloned.1.call-update) | async-done | bytes 33554448 | tf_op jit(solution)/shard_map/all_gather | solution.py:32
  248.1 1.3 convolution_bitcast_fusion.2
  249.4 2.1 fusion.6
  251.8 3.2 multiply_reduce_fusion.7
  254.9 12.4 %psum.63 = f32[128]{0:T(128)} all-reduce(f32[128]{0:T(128)} %get-tuple-element.523), channel_id=1, replica_groups=mesh['seq'=64,'head'=8] {'head'}, use_global_device_ids=true, to_apply=%region_5.6 | all-reduce | flops 128 | bytes 1024 | tf_op jit(solution)/shard_map/psum | solution.py:157
  268.5 1.9 fusion.41
  270.4 24.4 %all-reduce.5 = (f32[128]{0:T(128)}, f32[128,32]{0,1:T(8,128)}, f32[128,32]{0,1:T(8,128)}) all-reduce(f32[128]{0:T(128)} %get-tuple-element.524, f32[128,32]{0,1:T(8,128)} %fusion.92, f32[128,32]{0,1:T(8,128)} %fusion.41), channel_id=1, replica_groups=mesh['seq'=64,'head'=8] {'head'}, use_global_device_ids=true, to_apply=%region_8.9 | all-reduce | flops 8320 | bytes 66560 | tf_op jit(solution)/shard_map/psum | solution.py:168
  295.5 2.8 fusion.83
  298.4 1.2 copy.139
  299.6 1.9 convolution_bitcast_fusion.1
  301.5 2.0 copy.140
  303.7 1.3 broadcast_bitcast_fusion
  305.0 1.6 convolution_bitcast_fusion.9
  306.6 1.8 convolution_bitcast_fusion.6
  308.3 1.7 convolution_bitcast_fusion.8
  310.7 2.6 fusion.43
  313.3 1.5 convolution_multiply_fusion.3
  315.6 2.2 convolution_multiply_fusion.2
  317.9 280.0 %all-gather.8.cloned.1.call-done = f32[512,128,128]{2,1,0:T(8,128)} async-done(((f32[8,128,128]{2,1,0:T(8,128)}), f32[512,128,128]{2,1,0:T(8,128)}) %all-gather.8.cloned.1.call-update) | async-done | bytes 33554448 | tf_op jit(solution)/shard_map/all_gather | solution.py:32
  598.0 120.5 %while.21 = (s32[]{:T(128)}, f32[8,128,128]{2,1,0:T(8,128)S(1)}, s32[]{:T(128)}, f32[64,8]{1,0:T(8,128)}, f32[64,8,128,128]{3,2,1,0:T(8,128)}, /*index=5*/s32[]{:T(128)}, s32[]{:T(128)}, s32[]{:T(128)}, s32[]{:T(128)}) while((s32[]{:T(128)}, f32[8,128,128]{2,1,0:T(8,128)S(1)}, s32[]{:T(128)}, f32[64,8]{1,0:T(8,128)}, ...), condition=%wide.region_10.11_spmd, body=%wide.region_9.10_spmd.sunk | while | flops 262150 | bytes 1573115 | solution.py:41
  718.5 1.7 convolution_bitcast_fusion.10
  720.2 1.2 multiply_reduce_fusion.3
  721.4 1.7 convolution_add_fusion.2
  723.1 1.6 fusion.2
  724.9 1.4 add_multiply_fusion
  726.3 1.3 collective-permute-start.1
  728.0 4.0 collective-permute-done.1
  731.9 1.7 fusion.85
  733.6 1.2 fusion.65
  734.8 1.2 convolution_add_fusion.3
  736.1 1.9 collective-permute-start.2
  739.2 2.5 collective-permute-start.3
  742.7 2.1 collective-permute-done.3
  744.8 4.0 collective-permute-start.4
  748.8 1.6 maximum_multiply_fusion
  750.4 1.5 collective-permute-done.4
  757.6 1.7 fusion.7
  759.3 3.4 reduce-scatter.3.cloned.1.call-done
  762.7 162.7 %all-reduce.8.cloned.1.call-done = (f32[512,32]{0,1:T(8,128)}, f32[2,32,1024]{2,1,0:T(8,128)}, f32[1024,32]{0,1:T(8,128)}, f32[32,512]{1,0:T(8,128)}) async-done(((f32[512,32]{0,1:T(8,128)}, f32[2,32,1024]{2,1,0:T(8,128)}, f32[1024,32]{0,1:T(8,128)}, f32[32,512]{1,0:T(8,128)}), (f32[512,32]{0,1:T(8,128)}, f32[2,32,1024]{2,1,0:T(8,128)}, f32[1024,32]{0,1:T(8,128)}, ...) | async-done | bytes 524304 | tf_op jit(solution)/shard_map/psum | solution.py:215
  925.4 1.5 copy.191
  926.9 1.7 copy.192
  928.6 1.6 copy.193
  930.1 1.5 copy.194
  (224 shorter events, 144.4 us)
Async XLA Ops:
  7.2 167.5 %copy-start = (bf16[128,512]{1,0:T(8,128)(2,1)S(1)}, bf16[128,512]{1,0:T(8,128)(2,1)}, u32[]{:S(2)}) copy-start(bf16[128,512]{1,0:T(8,128)(2,1)} %param.32) | copy-start | bytes 393220
  7.2 307.7 %copy-start.4 = (bf16[128,128]{1,0:T(8,128)(2,1)S(1)}, bf16[128,128]{1,0:T(8,128)(2,1)}, u32[]{:S(2)}) copy-start(bf16[128,128]{1,0:T(8,128)(2,1)} %param.22) | copy-start | bytes 98308
  7.2 714.2 %copy-start.3 = (bf16[128,128]{1,0:T(8,128)(2,1)S(1)}, bf16[128,128]{1,0:T(8,128)(2,1)}, u32[]{:S(2)}) copy-start(bf16[128,128]{1,0:T(8,128)(2,1)} %param.23) | copy-start | bytes 98308
  7.2 744.7 %copy-start.5 = (bf16[128,512]{1,0:T(8,128)(2,1)S(1)}, bf16[128,512]{1,0:T(8,128)(2,1)}, u32[]{:S(2)}) copy-start(bf16[128,512]{1,0:T(8,128)(2,1)} %param.19) | copy-start | bytes 393220
  7.2 240.2 %all-gather.6.cloned.1.call-start = ((), (), s32[]{:S(2)}) async-start(), calls=%async_computation.4 | async-start | bytes 34078720 | tf_op jit(solution)/shard_map/all_gather | solution.py:32
  8.1 6.5 collective-permute-start
  13.2 3.5 copy-start.11
  13.2 3.5 copy-start.12
  13.2 3.5 copy-start.13
  13.2 3.5 copy-start.14
  14.2 159.3 %copy-start.10 = (f32[128,8]{0,1:T(8,128)}, f32[128,8]{0,1:T(8,128)S(1)}, u32[]{:S(2)}) copy-start(f32[128,8]{0,1:T(8,128)S(1)} %copy.132) | copy-start | bytes 12292
  14.5 182.8 %copy-start.7 = (f32[128,8]{0,1:T(8,128)}, f32[128,8]{0,1:T(8,128)S(1)}, u32[]{:S(2)}) copy-start(f32[128,8]{0,1:T(8,128)S(1)} %get-tuple-element.571) | copy-start | bytes 12292
  14.5 237.0 %copy-start.9 = (f32[128,8]{0,1:T(8,128)}, f32[128,8]{0,1:T(8,128)S(1)}, u32[]{:S(2)}) copy-start(f32[128,8]{0,1:T(8,128)S(1)} %get-tuple-element.572) | copy-start | bytes 12292
  19.1 578.8 %all-gather.8.cloned.1.call-start = ((), (), s32[]{:S(2)}) async-start(), calls=%async_computation.5 | async-start | bytes 34078720 | tf_op jit(solution)/shard_map/all_gather | solution.py:32
  173.6 78.0 %copy-start.8 = (f32[8,128]{1,0:T(8,128)}, f32[8,128]{1,0:T(8,128)S(1)}, u32[]{:S(2)}) copy-start(f32[8,128]{1,0:T(8,128)S(1)} %copy.129) | copy-start | bytes 12292
  247.5 0.6 copy-start.15
  251.7 43.8 %copy-start.2 = (f32[128,1024]{1,0:T(8,128)}, f32[128,1024]{1,0:T(8,128)S(1)}, u32[]{:S(2)}) copy-start(f32[128,1024]{1,0:T(8,128)S(1)} %copy.138) | copy-start | bytes 1572868
  254.9 43.4 %copy-start.1 = (f32[128,1024]{1,0:T(8,128)}, f32[128,1024]{1,0:T(8,128)S(1)}, u32[]{:S(2)}) copy-start(f32[128,1024]{1,0:T(8,128)S(1)} %get-tuple-element.558) | copy-start | bytes 1572868
  267.9 0.5 copy-start.16
  303.6 455.7 %reduce-scatter.5.cloned.1.call-start = ((), (), s32[]{:S(2)}) async-start(), calls=%async_computation.3 | async-start | bytes 73728 | tf_op jit(solution)/shard_map/reduce_scatter | solution.py:200
  313.3 284.6 %copy-start.6 = (f32[128,128]{1,0:T(8,128)}, f32[128,128]{1,0:T(8,128)S(1)}, u32[]{:S(2)}) copy-start(f32[128,128]{1,0:T(8,128)S(1)} %get-tuple-element.518) | copy-start | bytes 196612
  317.9 444.9 %reduce-scatter.3.cloned.1.call-start = ((), (), s32[]{:S(2)}) async-start(), calls=%async_computation.2 | async-start | bytes 73728 | tf_op jit(solution)/shard_map/reduce_scatter | solution.py:199
  726.3 5.6 collective-permute-start.1
  736.1 3.1 collective-permute-start.2
  738.8 186.6 %all-reduce.8.cloned.1.call-start = ((), (), s32[]{:S(2)}) async-start(), calls=%async_computation.6 | async-start | bytes 1048576 | tf_op jit(solution)/shard_map/psum | solution.py:215
  739.2 5.6 collective-permute-start.3
  744.8 7.1 collective-permute-start.4
Sparse Core Ops, SparseCore 0:
  19.2 228.1 all-gather.5
  303.7 294.1 all-gather.7
  601.3 30.7 reduce-scatter.4
  738.9 23.7 reduce-scatter.2
  767.4 158.0 all-reduce.7
